TPU v7x, 128 devices: a whole 4x4x4 slice. The times are simulated.
128 devices in a mesh: rcv: 8 (over x_hi, z), src: 16 (over y, x_lo, core).
Axes of the slice: x: 4 (x_hi: 2, x_lo: 2; x = x_hi * 2 + x_lo), y: 4, z: 4, core: 2. Of those that a mesh axis runs over, the one named last changes fastest.
Arguments:
- reflection: bfloat16 [2, 16384, 16384], P(None, 'rcv', 'src'), may hold values from -6 to 6
- green: bfloat16 [2, 16384, 512], P(None, 'rcv', 'src'), may hold values from -0.046875 to 0.046875
- tile_mask: int32 [64, 64], replicated, may hold values from 0 to 1, as said below
- reference_index: int32 [512], P(('rcv', 'src')), may hold values from 0 to 511
Outputs:
- aligned: float32 [512, 2, 512], P(('rcv', 'src'))
Inputs may be any that keep to these rules, and one draw needn't show every extreme that they name: `tile_mask`: entries below the diagonal are 0.
All inputs are finite; a program needn't handle non-finite values.
Results may differ from a plain program's by a relative error of at most 0.02.
Values may be sent and summed in bfloat16 or wider, within the bound.
No kernel may reach another device: no remote copies, remote signals or barrier semaphores. Data moves between devices by JAX's collectives and lax.ppermute only.
A program may use at most 128 MiB of HBM per device.

v0:
```python
import jax
import jax.numpy as jnp
from jax import lax
from jax.sharding import PartitionSpec as P

P_SIZE = 512
TILE = 256


def filled_up(lines, devices):
    spare = -lines.shape[0] % devices
    if not spare:
        return lines
    return jnp.concatenate([lines, jnp.zeros((spare, *lines.shape[1:]), lines.dtype)])


def spread(value, axis, root):
    lines = jnp.where(lax.axis_index(axis) == root, value, jnp.zeros_like(value)).reshape(
        -1, *value.shape[1:][-1:]
    )
    padded = filled_up(lines, lax.axis_size(axis))
    own = lax.psum_scatter(padded, axis, scatter_dimension=0, tiled=True)
    return lax.all_gather(own, axis, axis=0, tiled=True)[: len(lines)].reshape(value.shape)


def across(first, second, precision=None):
    return lax.dot_general(
        first,
        second,
        (((0,), (0,)), ((), ())),
        precision=precision,
        preferred_element_type=jnp.float32,
    )


def body(reflection, green, tile_mask, reference_index):
    rows_blk = reflection.shape[1]
    col_count = reflection.shape[2]
    rcv_index = lax.axis_index("rcv")
    src_index = lax.axis_index("src")
    green_block = lax.all_gather(green, "src", axis=2, tiled=True)
    src_per_rcv = lax.axis_size("src") // lax.axis_size("rcv")
    green_piece = lax.dynamic_slice_in_dim(
        green_block, src_index % src_per_rcv * col_count, col_count, 1
    )
    green_src = spread(green_piece, "rcv", src_index // src_per_rcv)
    row_tiles_count = rows_blk // TILE
    col_tiles_count = col_count // TILE
    tile_block = lax.dynamic_slice(
        tile_mask,
        (rcv_index * row_tiles_count, src_index * col_tiles_count),
        (row_tiles_count, col_tiles_count),
    )
    row_ids = rcv_index * row_tiles_count + jnp.arange(row_tiles_count)
    col_ids = src_index * col_tiles_count + jnp.arange(col_tiles_count)
    kept_tiles = tile_block == 1
    off_diag = kept_tiles & (row_ids[:, None] != col_ids[None, :])
    shaped = reflection.reshape(2, row_tiles_count, TILE, col_tiles_count, TILE)
    zero_value = jnp.zeros((), jnp.bfloat16)
    acquired = jnp.where(kept_tiles[None, :, None, :, None], shaped, zero_value).reshape(
        2, rows_blk, col_count
    )
    mirror_part = jnp.where(off_diag[None, :, None, :, None], shaped, zero_value).reshape(
        2, rows_blk, col_count
    )
    data_wide = jnp.concatenate([acquired[0], acquired[1], mirror_part[0], mirror_part[1]], axis=1)
    green_wide = jnp.concatenate([green_block[0], green_block[1]], axis=1)
    products = across(data_wide, green_wide)

    def quarter(row_slot, col_slot):
        return products[
            row_slot * col_count : (row_slot + 1) * col_count,
            col_slot * P_SIZE : (col_slot + 1) * P_SIZE,
        ]

    front_real = (quarter(0, 0) + quarter(1, 1)).astype(jnp.bfloat16)
    front_imag = (quarter(1, 0) - quarter(0, 1)).astype(jnp.bfloat16)
    back_real = (quarter(2, 0) - quarter(3, 1)).astype(jnp.bfloat16)
    back_imag = (quarter(3, 0) + quarter(2, 1)).astype(jnp.bfloat16)
    src_real = green_src[0]
    src_imag = green_src[1]
    green_stack = jnp.concatenate([src_real, src_imag], axis=0)
    mirror_left = jnp.concatenate(
        [
            jnp.concatenate([back_real, back_imag], axis=1),
            jnp.concatenate([back_imag, -back_real], axis=1),
        ],
        axis=0,
    )
    mirrored = across(green_stack, mirror_left)
    weights = jnp.concatenate(
        [
            jnp.concatenate([src_real, src_imag], axis=1),
            jnp.concatenate([-src_imag, src_real], axis=1),
        ],
        axis=0,
    )
    left_rows = jnp.concatenate([front_real, front_imag], axis=0)
    combined = across(left_rows, weights) + mirrored
    focal = lax.psum_scatter(combined, ("rcv", "src"), scatter_dimension=0, tiled=True)
    focal_real = focal[:, :P_SIZE]
    focal_imag = focal[:, P_SIZE:]
    chosen = jnp.arange(P_SIZE)[None, :] == reference_index[:, None]
    anchor_real = jnp.sum(jnp.where(chosen, focal_real, 0.0), axis=1)[:, None]
    anchor_imag = jnp.sum(jnp.where(chosen, focal_imag, 0.0), axis=1)[:, None]
    out_real = focal_real * anchor_real + focal_imag * anchor_imag
    out_imag = focal_imag * anchor_real - focal_real * anchor_imag
    return jnp.stack([out_real, out_imag], axis=1)


def solution(mesh):
    return jax.shard_map(
        body,
        mesh=mesh,
        in_specs=(P(None, "rcv", "src"), P(None, "rcv", "src"), P(), P(("rcv", "src"))),
        out_specs=P(("rcv", "src"), None, None),
        check_vma=False,
    )
```

profile of v0, /device:TPU:1, one launch (start us, length us, event | category | flops | bytes accessed | tf_op | source)
XLA Modules:
  0.0 371.1 jit_solution(2756795983004442803)
XLA Ops:
  6.5 1.9 copy.12
  8.6 14.5 %reshape.34 = bf16[2,8,256,4,256]{4,3,2,1,0:T(4,128)(2,1)} reshape(bf16[2,2048,1024]{2,1,0:T(8,128)(2,1)} %param.4) | data formatting | bytes 16777216 | tf_op jit(solution)/shard_map/reshape | solution.py:58
  23.9 26.3 %all-gather.3.cloned.1.call-done = bf16[2,2048,512]{1,0,2:T(2,128)(2,1)} async-done(((bf16[2,2048,32]{1,0,2:T(2,128)(2,1)}), bf16[2,2048,512]{1,0,2:T(2,128)(2,1)}) %all-gather.3.cloned.1.call-update) | async-done | bytes 4194320 | tf_op jit(solution)/shard_map/all_gather | solution.py:41
  50.1 4.4 %constant_dynamic-slice_fusion = bf16[2,1024,512]{1,0,2:T(2,128)(2,1)} fusion(bf16[2,2048,512]{1,0,2:T(2,128)(2,1)} %all-gather.3.cloned.1.call-done, s32[]{:T(128)S(6)} %select_n.49), kind=kLoop, calls=%fused_computation.52 | loop fusion | bytes 4194308 | tf_op jit(solution)/shard_map/dynamic_slice | solution.py:43
  54.5 4.7 %copy.19 = bf16[2,1024,512]{2,1,0:T(8,128)(2,1)S(1)} copy(bf16[2,1024,512]{1,0,2:T(2,128)(2,1)} %constant_dynamic-slice_fusion) | data formatting | bytes 4194304
  59.2 1.5 broadcast_select_fusion.2
  60.8 8.2 %broadcast_select_fusion.1 = (bf16[2,8,256,4,256]{4,3,2,1,0:T(4,128)(2,1)S(1)}, bf16[2,8,256,4,256]{4,3,2,1,0:T(4,128)(2,1)S(1)}) fusion(bf16[2,8,256,4,256]{4,3,2,1,0:T(4,128)(2,1)} %reshape.34, pred[8,4]{1,0:T(8,128)(4,1)S(1)} %get-tuple-element.10, pred[8,4]{1,0:T(8,128)(4,1)S(1)} %get-tuple-element.9), kind=kLoop, calls=%fused_computation.9 | loop fusion | flops 8388608 | bytes 25165888 | tf_op jit(solution)/shard_map/jit(_where)/select_n | solution.py:60
  68.9 6.2 %fusion.42 = (bf16[1,8,256,4,256]{4,3,2,1,0:T(4,128)(2,1)S(1)}, bf16[1,8,256,4,256]{4,3,2,1,0:T(4,128)(2,1)S(1)}, bf16[1,8,256,4,256]{4,3,2,1,0:T(4,128)(2,1)S(1)}, bf16[1,8,256,4,256]{4,3,2,1,0:T(4,128)(2,1)S(1)}) fusion(bf16[2,8,256,4,256]{4,3,2,1,0:T(4,128)(2,1)S(1)} %get-tuple-element.16, bf16[2,8,256,4,256]{4,3,2,1,0:T(4,128)(2,1)S(1)} %get-tuple-element.17), kind=kLoop, calls=%fused_computation.58 | loop fusion | bytes 33554432 | tf_op jit(solution)/shard_map/slice | solution.py:66
  75.1 3.0 copy.21
  78.1 3.0 copy.22
  81.1 3.0 copy.23
  84.1 3.0 copy.20
  87.1 6.9 %fusion.44 = (bf16[1,2048,512]{1,0,2:T(2,128)(2,1)}, bf16[1,2048,512]{1,0,2:T(2,128)(2,1)}) fusion(bf16[2,2048,512]{1,0,2:T(2,128)(2,1)S(1)} %copy-done), kind=kLoop, calls=%fused_computation.60 | loop fusion | bytes 8388608 | tf_op jit(solution)/shard_map/slice | solution.py:67
  94.1 9.0 %copy.17 = bf16[1,2048,512]{2,1,0:T(8,128)(2,1)S(1)} copy(bf16[1,2048,512]{1,0,2:T(2,128)(2,1)} %get-tuple-element.20) | data formatting | bytes 4194304
  103.0 10.5 %copy.18 = bf16[1,2048,512]{2,1,0:T(8,128)(2,1)} copy(bf16[1,2048,512]{1,0,2:T(2,128)(2,1)} %get-tuple-element.21) | data formatting | bytes 4194304
  113.5 20.8 %reduce-scatter.2.cloned.1.call-done = bf16[256,512]{1,0:T(8,128)(2,1)} async-done(((bf16[2048,512]{1,0:T(8,128)(2,1)}), bf16[256,512]{1,0:T(8,128)(2,1)}) %reduce-scatter.2.cloned.1.call-update) | async-done | bytes 262160 | tf_op jit(solution)/shard_map/reduce_scatter | solution.py:22
  134.6 27.2 %fusion = f32[4096,1024]{0,1:T(8,128)} fusion(bf16[2048,1024]{1,0:T(8,128)(2,1)} %bitcast.27, bf16[2048,1024]{1,0:T(8,128)(2,1)} %bitcast.26, bf16[2048,1024]{1,0:T(8,128)(2,1)} %bitcast.25, bf16[2048,1024]{1,0:T(8,128)(2,1)} %bitcast.28, bf16[2048,512]{1,0:T(8,128)(2,1)} %bitcast.30, bf16[2048,512]{1,0:T(8,128)(2,1)S(1)} %bitcast.29), kind=kOutput, calls=%fused_computation | convolution fusion | flops 17255366656 | bytes 37748736 | tf_op jit(solution)/shard_map/dot_general | solution.py:27
  161.8 2.8 fusion.40
  164.6 7.2 %fusion.27 = (bf16[1024,512]{0,1:T(8,128)(2,1)S(1)}, bf16[1024,512]{0,1:T(8,128)(2,1)}, bf16[1024,512]{0,1:T(8,128)(2,1)}) fusion(f32[4096,1024]{0,1:T(8,128)} %fusion), kind=kLoop, calls=%fused_computation.30 | loop fusion | flops 3145728 | bytes 15728640 | tf_op jit(solution)/shard_map/convert_element_type | solution.py:79
  171.8 18.9 %all-gather.5.cloned.1.call-done = bf16[2048,512]{1,0:T(8,128)(2,1)} async-done(((bf16[256,512]{1,0:T(8,128)(2,1)}), bf16[2048,512]{1,0:T(8,128)(2,1)}) %all-gather.5.cloned.1.call-update) | async-done | bytes 2097168 | tf_op jit(solution)/shard_map/all_gather | solution.py:23
  190.7 1.9 fusion.45
  192.8 2.4 fusion.11
  195.2 18.3 %fusion.34 = f32[512,1024]{1,0:T(8,128)} fusion(f32[512,1024]{1,0:T(8,128)S(1)} %fusion.11, bf16[2048,512]{1,0:T(8,128)(2,1)S(1)} %copy-done.1, bf16[1024,512]{0,1:T(8,128)(2,1)S(1)} %get-tuple-element.7, bf16[1024,512]{0,1:T(8,128)(2,1)S(1)} %get-tuple-element.11, bf16[1024,512]{0,1:T(8,128)(2,1)S(1)} %get-tuple-element.8), kind=kOutput, calls=%fused_computation.41 | convolution fusion | flops 2164785152 | bytes 9437184 | tf_op jit(solution)/shard_map/dot_general | solution.py:27
  213.5 148.7 %all-reduce.3.cloned.1.call-done = f32[512,1024]{1,0:T(8,128)} async-done(((f32[512,1024]{1,0:T(8,128)}), f32[512,1024]{1,0:T(8,128)}) %all-reduce.3.cloned.1.call-update) | async-done | bytes 2097168
  (25 shorter events, 3.8 us)
Async XLA Ops:
  6.5 43.6 %all-gather.3.cloned.1.call-start = ((), (), s32[]{:S(2)}) async-start(), calls=%async_computation.1 | async-start | bytes 4456448 | tf_op jit(solution)/shard_map/all_gather | solution.py:41
  8.5 125.9 %reduce-scatter.2.cloned.1.call-start = ((), (), s32[]{:S(2)}) async-start(), calls=%async_computation.2 | async-start | bytes 2359296 | tf_op jit(solution)/shard_map/reduce_scatter | solution.py:22
  60.7 130.0 %all-gather.5.cloned.1.call-start = ((), (), s32[]{:S(2)}) async-start(), calls=%async_computation.3 | async-start | bytes 2359296 | tf_op jit(solution)/shard_map/all_gather | solution.py:23
  84.1 3.0 copy-start
  134.4 227.8 %all-reduce.3.cloned.1.call-start = ((), (), s32[]{:S(2)}) async-start(), calls=%async_computation.4 | async-start | bytes 4194304
  190.7 1.9 copy-start.2
  190.7 2.2 copy-start.3
  192.8 2.4 copy-start.1
  195.2 167.0 %copy-start.4 = (s32[4]{0:T(128)S(1)}, s32[4]{0:T(128)}, u32[]{:S(2)}) copy-start(s32[4]{0:T(128)} %param.7) | copy-start | bytes 52
Sparse Core Ops, SparseCore 0:
  9.1 41.0 all-gather.2
  60.8 73.5 reduce-scatter.1
  136.7 53.8 all-gather.4
  213.6 148.4 all-reduce.2
where the time goes:
time: 372 us; the launch traced here: 371 us
  waiting for transfers between devices  215 us (58%)
  local copies, waits for them, and re-layouts  71 us (19%)
  matrix products  47.8 us (13%)
  other arithmetic  24 us (6%)
  between operations  13.2 us (4%)
    unnamed x5, waiting for transfers between devices  149 us
    dot_general x3, matrix products, across(): lax.dot_general(first, second, (((0,), (0,)), ((), ())), precision=precis...  47.8 us
    unnamed x18, local copies, waits for them, and re-layouts  38.4 us
    all_gather x1, waiting for transfers between devices, body(): green_block = lax.all_gather(green, 'src', axis=2, tiled=True)  26.3 us
    reduce_scatter x1, waiting for transfers between devices, spread(): own = lax.psum_scatter(padded, axis, scatter_dimension=0, tiled=True)  20.8 us
    all_gather x1, waiting for transfers between devices, spread(): lax.all_gather(own, axis, axis=0, tiled=True)[:len(lines)]  18.9 us
    reshape x1, local copies, waits for them, and re-layouts, body(): shaped = reflection.reshape(2, row_tiles_count, TILE, col_tiles_count, TILE)  14.5 us
    select_n x1, other arithmetic, body(): jnp.where(kept_tiles[None, :, None, :, None], shaped, zero_value)  8.16 us
  transfers between devices with their start and end apart: 4, of which 4 were waited for; matrix products, arithmetic and copies ran while one was open for 28% of the time, Pallas kernels for 0%

commit v1 on v0

--- a/solution.py
+++ b/solution.py
@@ -5,6 +5,13 @@
 
 P_SIZE = 512
 TILE = 256
+
+
+def all_by_exchange(block, name, dim):
+    size = lax.axis_size(name)
+    blocks = jnp.stack([block for _ in range(size)])
+    blocks = lax.all_to_all(blocks, name, split_axis=0, concat_axis=0)
+    return jnp.concatenate(blocks, axis=dim)
 
 
 def filled_up(lines, devices):
@@ -20,7 +27,7 @@
     )
     padded = filled_up(lines, lax.axis_size(axis))
     own = lax.psum_scatter(padded, axis, scatter_dimension=0, tiled=True)
-    return lax.all_gather(own, axis, axis=0, tiled=True)[: len(lines)].reshape(value.shape)
+    return all_by_exchange(own, axis, 0)[: len(lines)].reshape(value.shape)
 
 
 def across(first, second, precision=None):

time: 372 us -> 351 us (0.944)
  waiting for transfers between devices: 215 us -> 199 us
  matrix products: 47.8 us -> 33.8 us
  local copies, waits for them, and re-layouts: 71 us -> 76.1 us
  starting transfers between devices: 0.3 us -> 4.05 us
    all_gather x1 -> x0, waiting for transfers between devices: 18.9 us -> none  [spread(): lax.all_gather(own, axis, axis=0, tiled=True)[:len(lines)]]
    dot_general x3, matrix products: 47.8 us -> 33.8 us  [across(): lax.dot_general(first, second, (((0,), (0,)), ((), ())), precision=precis...]
    unnamed x5 -> x4, waiting for transfers between devices: 149 us -> 154 us
    all_to_all x0 -> x1, starting transfers between devices: none -> 3.78 us  [all_by_exchange(): blocks = lax.all_to_all(blocks, name, split_axis=0, concat_axis=0)]
    unnamed x18 -> x20, local copies, waits for them, and re-layouts: 38.4 us -> 40.9 us
  transfers between devices with their start and end apart: 4 -> 4, of which waited for: 4 -> 3; matrix products, arithmetic and copies ran while one was open for 28% -> 31% of each run, Pallas kernels for 0% -> 0%
where the time goes in v1:
time: 351 us; the launch traced here: 350 us
  waiting for transfers between devices  199 us (57%)
  local copies, waits for them, and re-layouts  76.1 us (22%)
  matrix products  33.8 us (10%)
  other arithmetic  23.1 us (7%)
  between operations  13.2 us (4%)
  starting transfers between devices  4.05 us (1%)
    unnamed x4, waiting for transfers between devices  154 us
    unnamed x20, local copies, waits for them, and re-layouts  40.9 us
    dot_general x3, matrix products, across(): lax.dot_general(first, second, (((0,), (0,)), ((), ())), precision=precis...  33.8 us
    all_gather x1, waiting for transfers between devices, body(): green_block = lax.all_gather(green, 'src', axis=2, tiled=True)  26.5 us
    reduce_scatter x1, waiting for transfers between devices, spread(): own = lax.psum_scatter(padded, axis, scatter_dimension=0, tiled=True)  19.1 us
    reshape x1, local copies, waits for them, and re-layouts, body(): shaped = reflection.reshape(2, row_tiles_count, TILE, col_tiles_count, TILE)  14.5 us
    select_n x1, other arithmetic, body(): jnp.where(kept_tiles[None, :, None, :, None], shaped, zero_value)  8.16 us
    convert_element_type x1, other arithmetic, body(): back_imag = (quarter(3, 0) + quarter(2, 1)).astype(jnp.bfloat16)  7.06 us
  transfers between devices with their start and end apart: 4, of which 3 were waited for; matrix products, arithmetic and copies ran while one was open for 31% of the time, Pallas kernels for 0%

profile of v1, /device:TPU:1, one launch (start us, length us, event | category | flops | bytes accessed | tf_op | source)
XLA Modules:
  0.0 349.8 jit_solution(15656305368218575176)
XLA Ops:
  6.5 1.9 copy.12
  8.6 14.5 %reshape.35 = bf16[2,8,256,4,256]{4,3,2,1,0:T(4,128)(2,1)} reshape(bf16[2,2048,1024]{2,1,0:T(8,128)(2,1)} %param.4) | data formatting | bytes 16777216 | tf_op jit(solution)/shard_map/reshape | solution.py:65
  23.9 26.5 %all-gather.2.cloned.1.call-done = bf16[2,2048,512]{1,0,2:T(2,128)(2,1)} async-done(((bf16[2,2048,32]{1,0,2:T(2,128)(2,1)}), bf16[2,2048,512]{1,0,2:T(2,128)(2,1)}) %all-gather.2.cloned.1.call-update) | async-done | bytes 4194320 | tf_op jit(solution)/shard_map/all_gather | solution.py:48
  50.3 4.4 %constant_dynamic-slice_fusion = bf16[2,1024,512]{1,0,2:T(2,128)(2,1)} fusion(bf16[2,2048,512]{1,0,2:T(2,128)(2,1)} %all-gather.2.cloned.1.call-done, s32[]{:T(128)S(6)} %select_n.49), kind=kLoop, calls=%fused_computation.55 | loop fusion | bytes 4194308 | tf_op jit(solution)/shard_map/dynamic_slice | solution.py:50
  54.7 4.7 %copy.19 = bf16[2,1024,512]{2,1,0:T(8,128)(2,1)S(1)} copy(bf16[2,1024,512]{1,0,2:T(2,128)(2,1)} %constant_dynamic-slice_fusion) | data formatting | bytes 4194304
  59.4 1.5 broadcast_select_fusion.2
  60.9 8.2 %broadcast_select_fusion.1 = (bf16[2,8,256,4,256]{4,3,2,1,0:T(4,128)(2,1)S(1)}, bf16[2,8,256,4,256]{4,3,2,1,0:T(4,128)(2,1)S(1)}) fusion(bf16[2,8,256,4,256]{4,3,2,1,0:T(4,128)(2,1)} %reshape.35, pred[8,4]{1,0:T(8,128)(4,1)S(1)} %get-tuple-element.10, pred[8,4]{1,0:T(8,128)(4,1)S(1)} %get-tuple-element.9), kind=kLoop, calls=%fused_computation.9 | loop fusion | flops 8388608 | bytes 25165888 | tf_op jit(solution)/shard_map/jit(_where)/select_n | solution.py:67
  69.1 6.2 %fusion.47 = (bf16[1,8,256,4,256]{4,3,2,1,0:T(4,128)(2,1)S(1)}, bf16[1,8,256,4,256]{4,3,2,1,0:T(4,128)(2,1)S(1)}, bf16[1,8,256,4,256]{4,3,2,1,0:T(4,128)(2,1)S(1)}, bf16[1,8,256,4,256]{4,3,2,1,0:T(4,128)(2,1)S(1)}) fusion(bf16[2,8,256,4,256]{4,3,2,1,0:T(4,128)(2,1)S(1)} %get-tuple-element.16, bf16[2,8,256,4,256]{4,3,2,1,0:T(4,128)(2,1)S(1)} %get-tuple-element.17), kind=kLoop, calls=%fused_computation.61 | loop fusion | bytes 33554432 | tf_op jit(solution)/shard_map/slice | solution.py:73
  75.3 3.0 copy.23
  78.3 3.0 copy.22
  81.3 3.0 copy.21
  84.3 3.0 copy.20
  87.3 7.0 %fusion.49 = (bf16[1,2048,512]{1,0,2:T(2,128)(2,1)}, bf16[1,2048,512]{1,0,2:T(2,128)(2,1)}) fusion(bf16[2,2048,512]{1,0,2:T(2,128)(2,1)S(1)} %copy-done), kind=kLoop, calls=%fused_computation.63 | loop fusion | bytes 8388608 | tf_op jit(solution)/shard_map/slice | solution.py:74
  94.2 10.5 %copy.18 = bf16[1,2048,512]{2,1,0:T(8,128)(2,1)} copy(bf16[1,2048,512]{1,0,2:T(2,128)(2,1)} %get-tuple-element.21) | data formatting | bytes 4194304
  104.7 10.5 %copy.17 = bf16[1,2048,512]{2,1,0:T(8,128)(2,1)} copy(bf16[1,2048,512]{1,0,2:T(2,128)(2,1)} %get-tuple-element.20) | data formatting | bytes 4194304
  115.2 19.1 %reduce-scatter.2.cloned.1.call-done = bf16[256,512]{1,0:T(8,128)(2,1)} async-done(((bf16[2048,512]{1,0:T(8,128)(2,1)}), bf16[256,512]{1,0:T(8,128)(2,1)}) %reduce-scatter.2.cloned.1.call-update) | async-done | bytes 262160 | tf_op jit(solution)/shard_map/reduce_scatter | solution.py:29
  134.3 2.4 stack.8
  136.8 3.8 %all-to-all-start = ((bf16[8,256,512]{2,1,0:T(8,128)(2,1)}), bf16[8,256,512]{2,1,0:T(8,128)(2,1)S(1)}, u32[]{:S(2)}, u32[]{:S(2)}) async-start(bf16[8,256,512]{2,1,0:T(8,128)(2,1)} %stack.8), calls=%async_computation.1 | async-start | bytes 4194304 | tf_op jit(solution)/shard_map/all_to_all | solution.py:13
  140.8 27.8 %fusion = f32[4096,1024]{0,1:T(8,128)} fusion(bf16[2048,1024]{1,0:T(8,128)(2,1)} %bitcast.27, bf16[2048,1024]{1,0:T(8,128)(2,1)} %bitcast.28, bf16[2048,1024]{1,0:T(8,128)(2,1)} %bitcast.29, bf16[2048,1024]{1,0:T(8,128)(2,1)} %bitcast.30, bf16[2048,512]{1,0:T(8,128)(2,1)} %bitcast.33, bf16[2048,512]{1,0:T(8,128)(2,1)} %bitcast.34), kind=kOutput, calls=%fused_computation | convolution fusion | flops 17255366656 | bytes 37748736 | tf_op jit(solution)/shard_map/dot_general | solution.py:34
  168.6 3.8 %fusion.45 = (bf16[1024,512]{0,1:T(8,128)(2,1)S(1)}, bf16[1024,512]{0,1:T(8,128)(2,1)}) fusion(f32[4096,1024]{0,1:T(8,128)} %fusion), kind=kLoop, calls=%fused_computation.60 | loop fusion | flops 1572864 | bytes 6291456 | tf_op jit(solution)/shard_map/neg | solution.py:93
  172.3 7.1 %fusion.27 = (bf16[1024,512]{0,1:T(8,128)(2,1)}, bf16[1024,512]{0,1:T(8,128)(2,1)}, bf16[1024,512]{0,1:T(8,128)(2,1)}) fusion(f32[4096,1024]{0,1:T(8,128)} %fusion), kind=kLoop, calls=%fused_computation.30 | loop fusion | flops 3145728 | bytes 15728640 | tf_op jit(solution)/shard_map/convert_element_type | solution.py:86
  181.0 2.3 fusion.11
  183.3 3.7 %fusion.37 = f32[512,1024]{1,0:T(8,128)} fusion(f32[512,1024]{1,0:T(8,128)S(1)} %fusion.11, bf16[1024,512]{0,1:T(8,128)(2,1)S(1)} %get-tuple-element.7, bf16[1024,512]{0,1:T(8,128)(2,1)S(1)} %copy-done.2, bf16[1024,512]{0,1:T(8,128)(2,1)S(1)} %copy-done.1, bf16[1024,512]{1,0:T(8,128)(2,1)S(1)} %bitcast.32, bf16[1024,512]{1,0:T(8,128)(2,1)S(1)} %bitcast.36), kind=kOutput, calls=%fused_computation.44 | convolution fusion | flops 2168979456 | bytes 9437184 | tf_op jit(solution)/shard_map/dot_general | solution.py:34
  187.1 153.8 %all-reduce.3.cloned.1.call-done = f32[512,1024]{1,0:T(8,128)} async-done(((f32[512,1024]{1,0:T(8,128)}), f32[512,1024]{1,0:T(8,128)}) %all-reduce.3.cloned.1.call-update) | async-done | bytes 2097168
  (28 shorter events, 5.0 us)
Async XLA Ops:
  6.5 43.8 %all-gather.2.cloned.1.call-start = ((), (), s32[]{:S(2)}) async-start(), calls=%async_computation.2 | async-start | bytes 4456448 | tf_op jit(solution)/shard_map/all_gather | solution.py:48
  8.5 125.8 %reduce-scatter.2.cloned.1.call-start = ((), (), s32[]{:S(2)}) async-start(), calls=%async_computation.3 | async-start | bytes 2359296 | tf_op jit(solution)/shard_map/reduce_scatter | solution.py:29
  84.3 3.0 copy-start
  136.8 42.6 %all-to-all-start = ((bf16[8,256,512]{2,1,0:T(8,128)(2,1)}), bf16[8,256,512]{2,1,0:T(8,128)(2,1)S(1)}, u32[]{:S(2)}, u32[]{:S(2)}) async-start(bf16[8,256,512]{2,1,0:T(8,128)(2,1)} %stack.8), calls=%async_computation.1 | async-start | bytes 4194304 | tf_op jit(solution)/shard_map/all_to_all | solution.py:13
  140.6 200.3 %all-reduce.3.cloned.1.call-start = ((), (), s32[]{:S(2)}) async-start(), calls=%async_computation.4 | async-start | bytes 4194304
  179.4 1.2 copy-start.3
  179.4 1.5 copy-start.4
  180.9 2.3 copy-start.1
  181.0 2.4 copy-start.2
  183.3 157.6 %copy-start.5 = (s32[4]{0:T(128)S(1)}, s32[4]{0:T(128)}, u32[]{:S(2)}) copy-start(s32[4]{0:T(128)} %param.7) | copy-start | bytes 52
Sparse Core Ops, SparseCore 0:
  9.1 41.2 all-gather.1
  61.0 73.2 reduce-scatter.1
  187.2 153.6 all-reduce.2
